TPU v7x, 256 devices: a whole 4x4x8 slice. The times are simulated.
256 devices in a mesh: grp: 8 (over y, core), seq: 32 (over x, z).
Axes of the slice: x: 4, y: 4, z: 8, core: 2. Of those that a mesh axis runs over, the one named last changes fastest.
Arguments:
- queries: float32 [262144, 256], P(('grp', 'seq')), may hold values from -6 to 6
- keys: float32 [262144, 256], P(('grp', 'seq')), may hold values from -6 to 6
- values: float32 [262144, 256], P(('grp', 'seq')), may hold values from -6 to 6
Outputs:
- mixed: float32 [262144, 256], P(('grp', 'seq'))
All inputs are finite; a program needn't handle non-finite values.
Results may differ from a plain program's by a relative error of at most 0.00018.
Values sent between devices are 32-bit elements; how exact they have to be, the bound alone decides.
A program may use at most 192 MiB of HBM per device.

v0:
```python
import jax
import jax.numpy as jnp
from jax import lax
from jax.sharding import PartitionSpec as P

HEADS = 2
HEAD = 128
BLOCK = 256
ITERS = 4


ridge = 1.0


def entering(value, axis, join, neutral):
    count, mine = (lax.axis_size(axis), lax.axis_index(axis))
    pieces = jax.tree.map(lambda part: lax.all_gather(part, axis), value)
    subtotal = jax.tree.map(
        lambda part, zero: jnp.full_like(part, 0) + jnp.asarray(zero, part.dtype), value, neutral
    )

    def hop(position, subtotal):
        longer = join(subtotal, jax.tree.map(lambda part: part[position], pieces))
        return jax.tree.map(lambda new, old: jnp.where(position < mine, new, old), longer, subtotal)

    return lax.fori_loop(0, count - 1, hop, subtotal)


def block_solve(qb, kb, vb, gram_pre, vk_pre):
    size = qb.shape[2]
    rows = lax.broadcasted_iota(jnp.int32, (size, size), 0)
    cols = lax.broadcasted_iota(jnp.int32, (size, size), 1)
    causal = (cols <= rows).astype(jnp.float32)
    best = lax.Precision.HIGHEST
    solved = jnp.zeros_like(qb)
    resid = qb
    direc = qb
    norm_now = jnp.sum(resid * resid, axis=-1, keepdims=True)
    for step in range(ITERS):
        own = jnp.einsum("hnta,hnab->hntb", direc, gram_pre, precision=best)
        apply_scores = jnp.einsum("hnta,hnsa->hnts", direc, kb, precision=best) * causal
        image = (
            own + jnp.einsum("hnts,hnsb->hntb", apply_scores, kb, precision=best) + ridge * direc
        )
        alpha = norm_now / jnp.sum(direc * image, axis=-1, keepdims=True)
        solved = solved + alpha * direc
        resid = resid - alpha * image
        norm_next = jnp.sum(resid * resid, axis=-1, keepdims=True)
        direc = resid + norm_next / norm_now * direc
        norm_now = norm_next
    outer = jnp.einsum("hntb,hnab->hnta", solved, vk_pre, precision=best)
    scores = jnp.einsum("hntb,hnsb->hnts", solved, kb, precision=best) * causal
    return outer + jnp.einsum("hnts,hnsa->hnta", scores, vb, precision=best)


def exclusive_sum(blocks):
    summed = jnp.cumsum(blocks, axis=1)
    return jnp.concatenate([jnp.zeros_like(blocks[:, :1]), summed[:, :-1]], axis=1)


def add_states(earlier, later):
    return (earlier[0] + later[0], earlier[1] + later[1])


def on_device(queries, keys, values):
    local_rows = queries.shape[0]
    count = local_rows // BLOCK
    best = lax.Precision.HIGHEST

    def split(arr):
        return arr.reshape(count, BLOCK, HEADS, HEAD).transpose(2, 0, 1, 3)

    qb, kb, vb = (split(queries), split(keys), split(values))
    gram_blk = jnp.einsum("hnsa,hnsb->hnab", kb, kb, precision=best)
    vk_blk = jnp.einsum("hnsa,hnsb->hnab", vb, kb, precision=best)
    own_states = (jnp.sum(gram_blk, axis=1), jnp.sum(vk_blk, axis=1))
    empty = jnp.zeros((HEADS, HEAD, HEAD), jnp.float32)
    before = entering(own_states, ("grp", "seq"), add_states, (empty, empty))
    gram_pre = before[0][:, None] + exclusive_sum(gram_blk)
    vk_pre = before[1][:, None] + exclusive_sum(vk_blk)
    outs = block_solve(qb, kb, vb, gram_pre, vk_pre)
    mixed = outs.transpose(1, 2, 0, 3).reshape(local_rows, HEADS * HEAD)
    start = (lax.axis_index("grp") * lax.axis_size("seq") + lax.axis_index("seq")) * local_rows
    place = (start + jnp.arange(local_rows, dtype=jnp.int32)).astype(jnp.float32)
    return mixed * jnp.sqrt(place + 1.0)[:, None]


def solution(mesh):
    return jax.shard_map(
        on_device,
        mesh=mesh,
        in_specs=(P(("grp", "seq"), None), P(("grp", "seq"), None), P(("grp", "seq"), None)),
        out_specs=P(("grp", "seq"), None),
        check_vma=False,
    )
```

profile of v0, /device:TPU:24, one launch (start us, length us, event | category | flops | bytes accessed | tf_op | source)
XLA Modules:
  0.0 635.4 jit_solution(7761331110546131487)
XLA Ops:
  6.5 1.8 reshape.72
  8.9 2.5 fusion.106
  11.5 2.5 fusion.105
  14.4 2.7 reshape.71
  17.1 1.5 copy.34
  19.0 3.2 fusion.57
  22.2 144.4 %all-gather.7.cloned.1.call-done = f32[512,128,128]{2,1,0:T(8,128)} async-done(((f32[2,128,128]{2,1,0:T(8,128)}), f32[512,128,128]{2,1,0:T(8,128)}) %all-gather.7.cloned.1.call-update) | async-done | bytes 33554448 | tf_op jit(solution)/shard_map/all_gather | solution.py:17
  166.5 153.0 %all-gather.5.cloned.1.call-done = f32[512,128,128]{2,1,0:T(8,128)} async-done(((f32[2,128,128]{2,1,0:T(8,128)}), f32[512,128,128]{2,1,0:T(8,128)}) %all-gather.5.cloned.1.call-update) | async-done | bytes 33554448 | tf_op jit(solution)/shard_map/all_gather | solution.py:17
  319.5 277.4 %while.16 = (s32[]{:T(128)}, f32[2,128,128]{2,1,0:T(8,128)S(1)}, f32[2,128,128]{2,1,0:T(8,128)S(1)}, s32[]{:T(128)}, f32[256,2,128,128]{3,2,1,0:T(8,128)}, /*ind...) while((s32[]{:T(128)}, f32[2,128,128]{2,1,0:T(8,128)S(1)}, f32[2,128,128]{2,1,0:T(8,128)S(1)}, ...), condition=%wide.region_4.5_spmd.clone, body=%wide.region_3.4_spmd.clone.sunk | while | flops 196612 | bytes 786541 | solution.py:26
  320.6 1.1 add_select_fusion.3
  322.8 1.1 add_select_fusion.3
  324.9 1.1 add_select_fusion.3
  326.0 1.1 add_select_fusion.3
  328.2 1.1 add_select_fusion.3
  330.4 1.1 add_select_fusion.3
  332.6 1.1 add_select_fusion.3
  333.6 1.1 add_select_fusion.3
  335.8 1.1 add_select_fusion.3
  598.5 2.6 fusion.66
  601.7 1.9 fusion.53
  603.6 1.1 fusion.82
  604.7 2.6 multiply_reduce_fusion.3
  607.8 1.9 fusion.49
  609.8 1.3 fusion.81
  611.1 2.6 multiply_reduce_fusion.1
  614.1 1.9 fusion.51
  616.1 1.1 fusion.80
  617.2 2.6 fusion.39
  620.3 1.9 fusion.55
  622.2 2.2 fusion.77
  624.4 2.1 fusion.36
  627.4 1.2 bitcast_multiply_fusion
  (283 shorter events, 267.4 us)
Async XLA Ops:
  6.5 1.8 copy-start.3
  6.5 160.0 %all-gather.7.cloned.1.call-start = ((), (), s32[]{:S(2)}) async-start(), calls=%async_computation.1 | async-start | bytes 33685504 | tf_op jit(solution)/shard_map/all_gather | solution.py:17
  8.9 5.0 copy-start
  11.4 308.1 %all-gather.5.cloned.1.call-start = ((), (), s32[]{:S(2)}) async-start(), calls=%async_computation | async-start | bytes 33685504 | tf_op jit(solution)/shard_map/all_gather | solution.py:17
  597.0 1.6 copy-start.2
  622.2 2.2 copy-start.1
Sparse Core Ops, SparseCore 0:
  11.6 154.9 all-gather.6
  170.2 149.2 all-gather.4
where the time goes:
time: 642 us; the launch traced here: 635 us
  waiting for transfers between devices  297 us (46%)
  other arithmetic  275 us (43%)
  matrix products  35.2 us (5%)
  between operations  13.7 us (2%)
  local copies, waits for them, and re-layouts  7.95 us (1%)
    all_gather x2, waiting for transfers between devices, entering(): pieces = jax.tree.map(lambda part: lax.all_gather(part, axis), value)  297 us
    select_n x255, other arithmetic, hop(): jnp.where(position < mine, new, old)  271 us
  transfers between devices with their start and end apart: 2, of which 2 were waited for; matrix products, arithmetic and copies ran while one was open for 2% of the time, Pallas kernels for 0%

commit v1 on v0

v1 whole, which is shorter than its diff:
```python
import functools

import jax
import jax.numpy as jnp
from jax import lax
from jax.experimental import pallas as pl
from jax.experimental.pallas import tpu as pltpu
from jax.sharding import PartitionSpec as P

HEADS = 2
HEAD = 128
BLOCK = 256
ITERS = 4
ZDIM = 8
F32 = jnp.float32
BF16 = jnp.bfloat16
MESH = pl.DeviceIdType.MESH


def halves(x):
    hi = x.astype(BF16)
    return hi, (x - hi.astype(F32)).astype(BF16)


def mm(a, b):
    return jnp.dot(a, b, preferred_element_type=F32)


def mmt(a, b):
    return lax.dot_general(a, b, (((0,), (0,)), ((), ())), preferred_element_type=F32)


def block_sums(k, v):
    k_hi, k_lo = halves(k)
    v_hi, v_lo = halves(v)
    wide = mmt(k_hi, jnp.concatenate([k_hi, k_lo, v_hi, v_lo], axis=1))
    rest = mmt(k_lo, jnp.concatenate([k_hi, v_hi], axis=1))
    gram = wide[:, :HEAD] + wide[:, HEAD : 2 * HEAD] + rest[:, :HEAD]
    state = wide[:, 2 * HEAD : 3 * HEAD] + wide[:, 3 * HEAD :] + rest[:, HEAD:]
    return gram, state


def scan_kernel(
    nz, k_hbm, v_hbm, e_ref, loc_hbm,
    kbuf, vbuf, loc, sums, zin, zpre, xin, gin, eout,
    ksem, vsem, locsem, zs, zr, xs, xr, gs, gr, es, er,
):
    g, s = lax.axis_index("grp"), lax.axis_index("seq")
    ng, nx = lax.axis_size("grp"), lax.axis_size("seq") // nz
    z, x = s % nz, s // nz
    blocks = kbuf.shape[0] // BLOCK
    rows = sums.shape[1]

    def along_z(d):
        return {"grp": g, "seq": x * nz + (z + d) % nz}

    def along_x(d):
        return {"grp": g, "seq": ((x + d) % nx) * nz + z}

    def along_g(d):
        return {"grp": (g + d) % ng, "seq": s}

    barrier = pltpu.get_barrier_semaphore()
    loads = []
    for b in range(blocks):
        at = pl.ds(b * BLOCK, BLOCK)
        loads.append((
            pltpu.make_async_copy(k_hbm.at[at], kbuf.at[at], ksem.at[b]),
            pltpu.make_async_copy(v_hbm.at[at], vbuf.at[at], vsem.at[b]),
        ))
        loads[-1][0].start()
        loads[-1][1].start()
    partners = [along_z(d) for d in range(1, nz)] + [along_x(d) for d in range(1, nx)] + [along_g(d) for d in range(1, ng)]
    for partner in partners:
        pl.semaphore_signal(barrier, inc=1, device_id=partner, device_id_type=MESH)

    total = [jnp.zeros((HEAD, HEAD), F32) for _ in range(2 * HEADS)]
    for b in range(blocks):
        loads[b][0].wait()
        loads[b][1].wait()
        for h in range(HEADS):
            at = (pl.ds(b * BLOCK, BLOCK), pl.ds(h * HEAD, HEAD))
            pair = block_sums(kbuf[at], vbuf[at])
            for i in range(2):
                loc[b, pl.ds((2 * h + i) * HEAD, HEAD), :] = total[2 * h + i]
                total[2 * h + i] = total[2 * h + i] + pair[i]
    per = HEAD // rows
    for i in range(2 * HEADS):
        sums[pl.ds(i * per, per)] = total[i].reshape(per, rows, HEAD)
    out_loc = pltpu.make_async_copy(loc, loc_hbm, locsem)
    out_loc.start()

    pl.semaphore_wait(barrier, len(partners))

    def zcopy(d):
        return pltpu.make_async_remote_copy(
            src_ref=sums.at[(z + d) % nz], dst_ref=zin.at[z], send_sem=zs.at[d], recv_sem=zr.at[d],
            device_id=along_z(d), device_id_type=MESH)

    def xcopy(d):
        return pltpu.make_async_remote_copy(
            src_ref=xin.at[x], dst_ref=xin.at[x], send_sem=xs.at[d], recv_sem=xr.at[d],
            device_id=along_x(d), device_id_type=MESH)

    def gcopy(d):
        return pltpu.make_async_remote_copy(
            src_ref=gin.at[g], dst_ref=gin.at[g], send_sem=gs.at[d], recv_sem=gr.at[d],
            device_id=along_g(d), device_id_type=MESH)

    def ecopy(d):
        return pltpu.make_async_remote_copy(
            src_ref=eout.at[(z + d) % nz], dst_ref=e_ref.at[z], send_sem=es.at[d], recv_sem=er.at[d],
            device_id=along_z(d), device_id_type=MESH)

    far_first = sorted(range(1, nz), key=lambda d: -min(d, nz - d))
    for d in far_first:
        zcopy(d).start()
    zin[z] = sums[z]
    for d in range(1, nz):
        zcopy(d).wait_recv()
    run = jnp.zeros((rows, HEAD), F32)
    for j in range(nz):
        zpre[j] = run
        run = run + zin[j]

    xin[x] = run
    for d in range(1, nx):
        xcopy(d).start()
    for d in range(1, nx):
        xcopy(d).wait_recv()
    before, whole = jnp.zeros((rows, HEAD), F32), jnp.zeros((rows, HEAD), F32)
    for j in range(nx):
        piece = xin[j]
        before = before + jnp.where(j < x, piece, 0.0)
        whole = whole + piece

    gin[g] = whole
    for d in range(1, ng):
        @pl.when(g + d < ng)
        def _():
            gcopy(d).start()
    for d in range(1, ng):
        @pl.when(g - d >= 0)
        def _():
            gcopy(d).wait_recv()
    before = before + lax.fori_loop(0, g, lambda j, acc: acc + gin[j], jnp.zeros((rows, HEAD), F32))

    for j in range(nz):
        eout[j] = zpre[j] + before
    for d in far_first:
        ecopy(d).start()
    e_ref[z] = eout[z]
    for d in range(1, nz):
        zcopy(d).wait_send()
    for d in range(1, nx):
        xcopy(d).wait_send()
    for d in range(1, ng):
        @pl.when(g + d < ng)
        def _():
            gcopy(d).wait_send()
    out_loc.wait()
    for d in range(1, nz):
        ecopy(d).wait_send()
        ecopy(d).wait_recv()


def entering(keys, values, nz):
    rows_local, width = keys.shape
    blocks = rows_local // BLOCK
    nx, ng = lax.axis_size("seq") // nz, lax.axis_size("grp")
    rows = 2 * HEADS * HEAD // nz
    any_space = pl.BlockSpec(memory_space=pl.ANY)
    dma = pltpu.SemaphoreType.DMA
    e, loc = pl.pallas_call(
        functools.partial(scan_kernel, nz),
        out_shape=(
            jax.ShapeDtypeStruct((nz, rows, HEAD), F32),
            jax.ShapeDtypeStruct((blocks, 2 * HEADS * HEAD, HEAD), F32),
        ),
        in_specs=[any_space, any_space],
        out_specs=(pl.BlockSpec(memory_space=pltpu.VMEM), any_space),
        scratch_shapes=[
            pltpu.VMEM((rows_local, width), F32),
            pltpu.VMEM((rows_local, width), F32),
            pltpu.VMEM((blocks, 2 * HEADS * HEAD, HEAD), F32),
            pltpu.VMEM((nz, rows, HEAD), F32),
            pltpu.VMEM((nz, rows, HEAD), F32),
            pltpu.VMEM((nz, rows, HEAD), F32),
            pltpu.VMEM((nx, rows, HEAD), F32),
            pltpu.VMEM((ng, rows, HEAD), F32),
            pltpu.VMEM((nz, rows, HEAD), F32),
            dma((blocks,)), dma((blocks,)), dma,
            dma((nz,)), dma((nz,)), dma((nx,)), dma((nx,)), dma((ng,)), dma((ng,)), dma((nz,)), dma((nz,)),
        ],
        compiler_params=pltpu.CompilerParams(collective_id=0, has_side_effects=True),
        name="scan",
    )(keys, values)
    return e.reshape(2 * HEADS * HEAD, HEAD), loc


def solve_kernel(q_ref, k_ref, v_ref, e_ref, loc_ref, out_ref):
    rows = lax.broadcasted_iota(jnp.int32, (BLOCK, BLOCK), 0)
    cols = lax.broadcasted_iota(jnp.int32, (BLOCK, BLOCK), 1)
    causal = cols <= rows
    probs = []
    for h in range(HEADS):
        lanes = pl.ds(h * HEAD, HEAD)
        q, k, v = q_ref[:, lanes], k_ref[:, lanes], v_ref[:, lanes]
        at = [pl.ds((2 * h + i) * HEAD, HEAD) for i in range(2)]
        gram = e_ref[at[0], :] + loc_ref[0, at[0], :]
        state = e_ref[at[1], :] + loc_ref[0, at[1], :]
        kt_hi, kt_lo = halves(k.T)
        gram_hi, gram_lo = halves(gram)
        state_hi, state_lo = halves(state)
        probs.append(dict(
            q=q, top=jnp.concatenate([gram_hi, kt_hi], axis=1), low=jnp.concatenate([gram_lo, kt_lo], axis=1),
            top_end=jnp.concatenate([state_hi, kt_hi], axis=1), low_end=jnp.concatenate([state_lo, kt_lo], axis=1),
            k=halves(k), v=halves(v)))

    def spread(p, top, low, right):
        p_hi, p_lo = halves(p)
        t = mm(jnp.concatenate([p_hi, p_lo], axis=1), jnp.concatenate([top, top], axis=0)) + mm(p_hi, low)
        scores = jnp.where(causal, t[:, HEAD:], 0.0)
        s_hi, s_lo = halves(scores)
        u = mm(s_hi, jnp.concatenate(right, axis=1))
        return t[:, :HEAD] + (u[:, :HEAD] + u[:, HEAD:] + mm(s_lo, right[0]))

    def dots(a, b):
        return jnp.sum(a * b, axis=-1, keepdims=True)

    state = [dict(x=jnp.zeros_like(p["q"]), r=p["q"], p=p["q"], rr=dots(p["q"], p["q"])) for p in probs]
    for step in range(ITERS):
        images = [spread(st["p"], pr["top"], pr["low"], pr["k"]) + st["p"] for st, pr in zip(state, probs)]
        for st, image in zip(state, images):
            alpha = st["rr"] / dots(st["p"], image)
            st["x"] = st["x"] + alpha * st["p"]
            if step < ITERS - 1:
                st["r"] = st["r"] - alpha * image
                new = dots(st["r"], st["r"])
                st["p"] = st["r"] + new / st["rr"] * st["p"]
                st["rr"] = new
    first = (lax.axis_index("grp") * lax.axis_size("seq") + lax.axis_index("seq")) * (pl.num_programs(0) * BLOCK)
    first = first + pl.program_id(0) * BLOCK
    place = (first + lax.broadcasted_iota(jnp.int32, (BLOCK, HEAD), 0)).astype(F32)
    scale = jnp.sqrt(place + 1.0)
    for h, (st, pr) in enumerate(zip(state, probs)):
        out_ref[:, pl.ds(h * HEAD, HEAD)] = spread(st["x"], pr["top_end"], pr["low_end"], pr["v"]) * scale


def solve(queries, keys, values, e, loc):
    rows_local, width = queries.shape
    tok = pl.BlockSpec((BLOCK, width), lambda n: (n, 0))
    return pl.pallas_call(
        solve_kernel,
        grid=(rows_local // BLOCK,),
        out_shape=jax.ShapeDtypeStruct((rows_local, width), F32),
        in_specs=[tok, tok, tok, pl.BlockSpec(e.shape, lambda n: (0, 0)), pl.BlockSpec((1,) + loc.shape[1:], lambda n: (n, 0, 0))],
        out_specs=tok,
        name="solve",
    )(queries, keys, values, e, loc)


def on_device(queries, keys, values):
    e, loc = entering(keys, values, ZDIM)
    return solve(queries, keys, values, e, loc)


def solution(mesh):
    return jax.shard_map(
        on_device,
        mesh=mesh,
        in_specs=(P(("grp", "seq"), None), P(("grp", "seq"), None), P(("grp", "seq"), None)),
        out_specs=P(("grp", "seq"), None),
        check_vma=False,
    )
```

time: 642 us -> 47.7 us (0.07)
  waiting for transfers between devices: 297 us -> 0 us
  other arithmetic: 275 us -> 0 us
  Pallas kernels: 0 us -> 47.5 us
  matrix products: 35.2 us -> 0 us
  between operations: 13.7 us -> 0.01 us
  local copies, waits for them, and re-layouts: 7.95 us -> 0 us
    all_gather x2 -> x0, waiting for transfers between devices: 297 us -> none  [entering(): pieces = jax.tree.map(lambda part: lax.all_gather(part, axis), value)]
    select_n x255 -> x0, other arithmetic: 271 us -> none  [hop(): jnp.where(position < mine, new, old)]
    pallas_call x0 -> x2, Pallas kernels: none -> 47.5 us  [the longest x1 32.9 us: entering(): pl.pallas_call(functools.partial(scan_kernel, nz), out_shape=(jax.ShapeDt...]
    dot_general x17 -> x0, matrix products: 35.2 us -> none  [the longest x4 10.4 us: block_solve(): jnp.einsum('hnts,hnsb->hntb', apply_scores, kb, precision=best)]
    reshape x4 -> x0, local copies, waits for them, and re-layouts: 6.55 us -> none  [split(): return arr.reshape(count, BLOCK, HEADS, HEAD).transpose(2, 0, 1, 3)]
  transfers between devices with their start and end apart: 2 -> 0, of which waited for: 2 -> 0; matrix products, arithmetic and copies ran while one was open for 2% -> 0% of each run, Pallas kernels for 0% -> 0%
where the time goes in v1:
time: 47.7 us; the launch traced here: 47.5 us
  Pallas kernels  47.5 us (100%)
    pallas_call x1, Pallas kernels, entering(): pl.pallas_call(functools.partial(scan_kernel, nz), out_shape=(jax.ShapeDt...  32.9 us
    pallas_call x1, Pallas kernels, solve(): pl.pallas_call(solve_kernel, grid=(rows_local // BLOCK,), out_shape=jax.S...  14.5 us

profile of v1, /device:TPU:24, one launch (start us, length us, event | category | flops | bytes accessed | tf_op | source)
XLA Modules:
  0.0 47.5 jit_solution(2648532911897991997)
XLA Ops:
  0.0 32.9 %scan.1 = (f32[8,64,128]{2,1,0:T(8,128)}, f32[4,512,128]{2,1,0:T(8,128)}) custom-call(f32[1024,256]{1,0:T(8,128)} %k_ref.1, f32[1024,256]{1,0:T(8,128)} %v_ref.1), custom_call_target="tpu_custom_call" | custom-call | tf_op jit(solution)/shard_map/scan/pallas_call | solution.py:174
  33.0 14.5 %solve.1 = f32[1024,256]{1,0:T(8,128)} custom-call(f32[1024,256]{1,0:T(8,128)} %q_ref.1, f32[1024,256]{1,0:T(8,128)} %k_ref.1, f32[1024,256]{1,0:T(8,128)} %v_ref.1, f32[512,128]{1,0:T(8,128)} %bitcast.1, f32[4,512,128]{2,1,0:T(8,128)} %get-tuple-element.8.loc_ref), custom_call_target="tpu_custom_call" | custom-call | tf_op jit(solution)/shard_map/solve/pallas_call | solution.py:253

commit v2 on v0

v2 whole, which is shorter than its diff:
```python
import functools

import jax
import jax.numpy as jnp
from jax import lax
from jax.experimental import pallas as pl
from jax.experimental.pallas import tpu as pltpu
from jax.sharding import PartitionSpec as P

HEADS = 2
HEAD = 128
BLOCK = 256
ITERS = 4
ZDIM = 8
GROUP = 512
CHANS = 2 * HEADS
F32 = jnp.float32
BF16 = jnp.bfloat16
MESH = pl.DeviceIdType.MESH


def halves(x):
    hi = x.astype(BF16)
    return hi, (x - hi.astype(F32)).astype(BF16)


def cat(*xs, axis):
    return jnp.concatenate(xs, axis=axis)


def mm(a, b):
    return jnp.dot(a, b, preferred_element_type=F32)


def mmt(a, b):
    return lax.dot_general(a, b, (((0,), (0,)), ((), ())), preferred_element_type=F32)


def narrow(a_hi, a_lo, b_hi, b_lo):
    right = cat(cat(b_hi, b_lo, axis=1), cat(b_hi, jnp.zeros_like(b_lo), axis=1), axis=0)
    t = mm(cat(a_hi, a_lo, axis=1), right)
    return t[:, :HEAD] + t[:, HEAD:]


def scores_of(a_hi, a_lo, kt_hi, kt_lo):
    return mm(cat(a_hi, a_lo, axis=1), cat(kt_hi, kt_hi, axis=0)) + mm(a_hi, kt_lo)


def weighted(s, b_hi, b_lo):
    s_hi, s_lo = halves(s)
    t = mm(s_hi, cat(b_hi, b_lo, axis=1))
    return t[:, :HEAD] + t[:, HEAD:] + mm(s_lo, b_hi)


def causal_mask():
    rows = lax.broadcasted_iota(jnp.int32, (BLOCK, BLOCK), 0)
    cols = lax.broadcasted_iota(jnp.int32, (BLOCK, BLOCK), 1)
    return cols <= rows


def lanes(h):
    return pl.ds(h * HEAD, HEAD)


def scan_kernel(
    nz, q_hbm, k_hbm, v_hbm, e_ref, loc_ref, q_ref, img_ref, s_ref, kt_ref, kh_ref, vh_ref,
    kbuf, vbuf, sums, zin, zpre, xin, gin, eout,
    qsem, ksem, vsem, zs, zr, xs, xr, gs, gr, es, er,
):
    g, s = lax.axis_index("grp"), lax.axis_index("seq")
    ng, nx = lax.axis_size("grp"), lax.axis_size("seq") // nz
    z, x = s % nz, s // nz
    blocks = kbuf.shape[0] // BLOCK
    rows = HEAD // nz

    def along_z(d):
        return {"grp": g, "seq": x * nz + (z + d) % nz}

    def along_x(d):
        return {"grp": g, "seq": ((x + d) % nx) * nz + z}

    def along_g(d):
        return {"grp": (g + d) % ng, "seq": s}

    loads = {}
    for h in range(HEADS):
        for b in range(blocks):
            at = (pl.ds(b * BLOCK, BLOCK), lanes(h))
            loads[h, b] = (
                pltpu.make_async_copy(k_hbm.at[at], kbuf.at[at], ksem.at[h, b]),
                pltpu.make_async_copy(v_hbm.at[at], vbuf.at[at], vsem.at[h, b]),
            )
            loads[h, b][0].start()
            loads[h, b][1].start()
    q_load = pltpu.make_async_copy(q_hbm, q_ref, qsem)
    q_load.start()
    barrier = pltpu.get_barrier_semaphore()
    partners = [along_z(d) for d in range(1, nz)] + [along_x(d) for d in range(1, nx)] + [along_g(d) for d in range(1, ng)]
    for partner in partners:
        pl.semaphore_signal(barrier, inc=1, device_id=partner, device_id_type=MESH)

    def remote(src, dst, send, recv, to):
        return pltpu.make_async_remote_copy(
            src_ref=src, dst_ref=dst, send_sem=send, recv_sem=recv, device_id=to, device_id_type=MESH)

    def zcopy(c, d):
        return remote(sums.at[c, (z + d) % nz], zin.at[c, z], zs.at[c, d], zr.at[c, d], along_z(d))

    def xcopy(c, d):
        return remote(xin.at[c, x], xin.at[c, x], xs.at[c, d], xr.at[c, d], along_x(d))

    def gcopy(c, d):
        return remote(gin.at[c, g], gin.at[c, g], gs.at[c, d], gr.at[c, d], along_g(d))

    def ecopy(c, d):
        return remote(eout.at[c, (z + d) % nz], e_ref.at[c, z], es.at[c, d], er.at[c, d], along_z(d))

    far_first = sorted(range(1, nz), key=lambda d: -min(d, nz - d))

    for h in range(HEADS):
        total = [jnp.zeros((HEAD, HEAD), F32) for _ in range(2)]
        for b in range(blocks):
            loads[h, b][0].wait()
            loads[h, b][1].wait()
            at = (pl.ds(b * BLOCK, BLOCK), lanes(h))
            k_hi, k_lo = halves(kbuf[at])
            v_hi, v_lo = halves(vbuf[at])
            kh_ref[0, b, h] = k_hi
            kh_ref[1, b, h] = k_lo
            vh_ref[0, b, h] = v_hi
            vh_ref[1, b, h] = v_lo
            wide = mmt(k_hi, cat(k_hi, k_lo, v_hi, v_lo, axis=1))
            rest = mmt(k_lo, cat(k_hi, v_hi, axis=1))
            for i in range(2):
                loc_ref[b, pl.ds((2 * h + i) * HEAD, HEAD), :] = total[i]
                base = 2 * i * HEAD
                total[i] = total[i] + (wide[:, base : base + HEAD] + wide[:, base + HEAD : base + 2 * HEAD] + rest[:, i * HEAD : (i + 1) * HEAD])
        for i in range(2):
            sums[2 * h + i] = total[i].reshape(nz, rows, HEAD)
        if h == 0:
            pl.semaphore_wait(barrier, len(partners))
        for i in range(2):
            for d in far_first:
                zcopy(2 * h + i, d).start()
            zin[2 * h + i, z] = sums[2 * h + i, z]

    q_load.wait()

    @pl.loop(0, blocks)
    def _(b):
        causal = causal_mask()
        row = pl.ds(pl.multiple_of(b * BLOCK, BLOCK), BLOCK)
        for h in range(HEADS):
            q = q_ref[row, lanes(h)]
            q_hi, q_lo = halves(q)
            kt_hi, kt_lo = halves(kbuf[row, lanes(h)].T)
            kt_ref[0, b, h] = kt_hi
            kt_ref[1, b, h] = kt_lo
            scores = jnp.where(causal, scores_of(q_hi, q_lo, kt_hi, kt_lo), 0.0)
            s_ref[b, h] = scores
            gram = halves(loc_ref[b, pl.ds(2 * h * HEAD, HEAD), :])
            near = weighted(scores, kh_ref[0, b, h], kh_ref[1, b, h])
            img_ref[row, lanes(h)] = near + narrow(q_hi, q_lo, *gram) + q

    zero = jnp.zeros((rows, HEAD), F32)
    held = {}

    def after_z(c):
        for d in range(1, nz):
            zcopy(c, d).wait_recv()
        run = zero
        for j in range(nz):
            zpre[c, j] = run
            run = run + zin[c, j]
        xin[c, x] = run
        for d in range(1, nx):
            xcopy(c, d).start()

    def after_x(c):
        for d in range(1, nx):
            xcopy(c, d).wait_recv()
        before, whole = zero, zero
        for j in range(nx):
            piece = xin[c, j]
            before = before + jnp.where(j < x, piece, 0.0)
            whole = whole + piece
        held[c] = before
        gin[c, g] = whole
        for d in range(1, ng):
            @pl.when(g + d < ng)
            def _():
                gcopy(c, d).start()

    def after_g(c):
        for d in range(1, ng):
            @pl.when(g - d >= 0)
            def _():
                gcopy(c, d).wait_recv()
        before = held[c] + lax.fori_loop(0, g, lambda j, acc: acc + gin[c, j], zero)
        for j in range(nz):
            eout[c, j] = zpre[c, j] + before
        for d in far_first:
            ecopy(c, d).start()
        e_ref[c, z] = eout[c, z]

    lag_x, lag_g = 2, 3
    for t in range(CHANS + lag_x + lag_g):
        if t < CHANS:
            after_z(t)
        if 0 <= t - lag_x < CHANS:
            after_x(t - lag_x)
        if 0 <= t - lag_x - lag_g < CHANS:
            after_g(t - lag_x - lag_g)

    for c in range(CHANS):
        for d in range(1, nz):
            zcopy(c, d).wait_send()
        for d in range(1, nx):
            xcopy(c, d).wait_send()
        for d in range(1, ng):
            @pl.when(g + d < ng)
            def _():
                gcopy(c, d).wait_send()
    for c in range(CHANS):
        for d in range(1, nz):
            ecopy(c, d).wait_send()
            ecopy(c, d).wait_recv()


def entering(queries, keys, values, nz):
    tokens, width = keys.shape
    blocks = tokens // BLOCK
    nx, ng = lax.axis_size("seq") // nz, lax.axis_size("grp")
    rows = HEAD // nz
    hbm = pl.BlockSpec(memory_space=pltpu.HBM)
    vmem = pl.BlockSpec(memory_space=pltpu.VMEM)
    dma = pltpu.SemaphoreType.DMA
    outs = (
        pltpu.VMEM((CHANS, nz, rows, HEAD), F32),
        pltpu.VMEM((blocks, CHANS * HEAD, HEAD), F32),
        pltpu.VMEM((tokens, width), F32),
        pltpu.VMEM((tokens, width), F32),
        pltpu.VMEM((blocks, HEADS, BLOCK, BLOCK), F32),
        pltpu.VMEM((2, blocks, HEADS, HEAD, BLOCK), BF16),
        pltpu.VMEM((2, blocks, HEADS, BLOCK, HEAD), BF16),
        pltpu.VMEM((2, blocks, HEADS, BLOCK, HEAD), BF16),
    )
    e, loc, *rest = pl.pallas_call(
        functools.partial(scan_kernel, nz),
        out_shape=outs,
        in_specs=[hbm] * 3,
        out_specs=(vmem,) * len(outs),
        scratch_shapes=[
            pltpu.VMEM((tokens, width), F32),
            pltpu.VMEM((tokens, width), F32),
            pltpu.VMEM((CHANS, nz, rows, HEAD), F32),
            pltpu.VMEM((CHANS, nz, rows, HEAD), F32),
            pltpu.VMEM((CHANS, nz, rows, HEAD), F32),
            pltpu.VMEM((CHANS, nx, rows, HEAD), F32),
            pltpu.VMEM((CHANS, ng, rows, HEAD), F32),
            pltpu.VMEM((CHANS, nz, rows, HEAD), F32),
            dma, dma((HEADS, blocks)), dma((HEADS, blocks)),
            dma((CHANS, nz)), dma((CHANS, nz)), dma((CHANS, nx)), dma((CHANS, nx)),
            dma((CHANS, ng)), dma((CHANS, ng)), dma((CHANS, nz)), dma((CHANS, nz)),
        ],
        compiler_params=pltpu.CompilerParams(collective_id=0, has_side_effects=True, vmem_limit_bytes=57_500_000),
        name="scan",
    )(queries, keys, values)
    return e.reshape(CHANS * HEAD, HEAD), loc, *rest


def solve_kernel(e_ref, loc_ref, q_ref, img_ref, s_ref, kt_ref, kh_ref, vh_ref, out_ref):
    causal = causal_mask()

    def dots(a, b):
        return jnp.sum(a * b, axis=-1, keepdims=True)

    per = GROUP // BLOCK
    state = []
    for c in range(per):
        for h in range(HEADS):
            n = pl.program_id(0) * per + c
            row = pl.ds(pl.multiple_of(n * BLOCK, BLOCK), BLOCK)
            at = [pl.ds((2 * h + i) * HEAD, HEAD) for i in range(2)]
            enter = e_ref[at[0], :]
            q = q_ref[row, lanes(h)]
            state.append(dict(
                c=c, h=h, n=n, row=row, enter=halves(enter), gram=halves(enter + loc_ref[n, at[0], :]),
                state=halves(e_ref[at[1], :] + loc_ref[n, at[1], :]), x=None, r=q, p=q, rr=dots(q, q), acc=None))
    for step in range(ITERS):
        images, scores = [], []
        for st in state:
            n, h = st["n"], st["h"]
            p_hi, p_lo = halves(st["p"])
            if step == 0:
                scores.append(s_ref[n, h])
                images.append(narrow(p_hi, p_lo, *st["enter"]) + img_ref[st["row"], lanes(h)])
            else:
                sc = jnp.where(causal, scores_of(p_hi, p_lo, kt_ref[0, n, h], kt_ref[1, n, h]), 0.0)
                scores.append(sc)
                images.append(narrow(p_hi, p_lo, *st["gram"]) + weighted(sc, kh_ref[0, n, h], kh_ref[1, n, h]) + st["p"])
        for st, image, sc in zip(state, images, scores):
            alpha = st["rr"] / dots(st["p"], image)
            st["x"] = alpha * st["p"] if step == 0 else st["x"] + alpha * st["p"]
            st["acc"] = alpha * sc if step == 0 else st["acc"] + alpha * sc
            if step < ITERS - 1:
                st["r"] = st["r"] - alpha * image
                new = dots(st["r"], st["r"])
                st["p"] = st["r"] + new / st["rr"] * st["p"]
                st["rr"] = new
    first = lax.axis_index("grp") * lax.axis_size("seq") + lax.axis_index("seq")
    first = (first * pl.num_programs(0) + pl.program_id(0)) * GROUP
    for st in state:
        n, h = st["n"], st["h"]
        place = (first + st["c"] * BLOCK + lax.broadcasted_iota(jnp.int32, (BLOCK, HEAD), 0)).astype(F32)
        out = narrow(*halves(st["x"]), *st["state"]) + weighted(st["acc"], vh_ref[0, n, h], vh_ref[1, n, h])
        out_ref[pl.ds(st["c"] * BLOCK, BLOCK), lanes(h)] = out * jnp.sqrt(place + 1.0)


def solve(*parts):
    tokens, width = parts[2].shape
    return pl.pallas_call(
        solve_kernel,
        grid=(tokens // GROUP,),
        out_shape=jax.ShapeDtypeStruct((tokens, width), F32),
        in_specs=[pl.BlockSpec(memory_space=pltpu.VMEM)] * len(parts),
        out_specs=pl.BlockSpec((GROUP, width), lambda n: (n, 0)),
        compiler_params=pltpu.CompilerParams(vmem_limit_bytes=24 * 2**20),
        name="solve",
    )(*parts)


def on_device(queries, keys, values):
    return solve(*entering(queries, keys, values, ZDIM))


def solution(mesh):
    return jax.shard_map(
        on_device,
        mesh=mesh,
        in_specs=(P(("grp", "seq"), None), P(("grp", "seq"), None), P(("grp", "seq"), None)),
        out_specs=P(("grp", "seq"), None),
        check_vma=False,
    )
```

time: 642 us -> 41.1 us (0.06)
  waiting for transfers between devices: 297 us -> 0 us
  other arithmetic: 275 us -> 0 us
  Pallas kernels: 0 us -> 40.9 us
  matrix products: 35.2 us -> 0 us
  between operations: 13.7 us -> 0.01 us
  local copies, waits for them, and re-layouts: 7.95 us -> 0 us
    all_gather x2 -> x0, waiting for transfers between devices: 297 us -> none  [entering(): pieces = jax.tree.map(lambda part: lax.all_gather(part, axis), value)]
    select_n x255 -> x0, other arithmetic: 271 us -> none  [hop(): jnp.where(position < mine, new, old)]
    pallas_call x0 -> x2, Pallas kernels: none -> 40.9 us  [the longest x1 31 us: entering(): pl.pallas_call(functools.partial(scan_kernel, nz), out_shape=outs, in_spe...]
    dot_general x17 -> x0, matrix products: 35.2 us -> none  [the longest x4 10.4 us: block_solve(): jnp.einsum('hnts,hnsb->hntb', apply_scores, kb, precision=best)]
    reshape x4 -> x0, local copies, waits for them, and re-layouts: 6.55 us -> none  [split(): return arr.reshape(count, BLOCK, HEADS, HEAD).transpose(2, 0, 1, 3)]
  transfers between devices with their start and end apart: 2 -> 0, of which waited for: 2 -> 0; matrix products, arithmetic and copies ran while one was open for 2% -> 0% of each run, Pallas kernels for 0% -> 0%
where the time goes in v2:
time: 41.1 us; the launch traced here: 40.9 us
  Pallas kernels  40.9 us (100%)
    pallas_call x1, Pallas kernels, entering(): pl.pallas_call(functools.partial(scan_kernel, nz), out_shape=outs, in_spe...  31 us
    pallas_call x1, Pallas kernels, solve(): pl.pallas_call(solve_kernel, grid=(tokens // GROUP,), out_shape=jax.Shape...  9.88 us

profile of v2, /device:TPU:24, one launch (start us, length us, event | category | flops | bytes accessed | tf_op | source)
XLA Modules:
  0.0 40.9 jit_solution(12397171416104670995)
XLA Ops:
  0.0 31.0 %scan.1 = (f32[4,8,16,128]{3,2,1,0:T(8,128)S(1)}, f32[4,512,128]{2,1,0:T(8,128)S(1)}, f32[1024,256]{1,0:T(8,128)S(1)}, f32[1024,256]{1,0:T(8,128)S(1)}, f32[4,2,...) custom-call(f32[1024,256]{1,0:T(8,128)} %q_hbm.1, ...), custom_call_target="tpu_custom_call" | custom-call | tf_op jit(solution)/shard_map/scan/pallas_call | solution.py:248
  31.0 9.9 %solve.1 = f32[1024,256]{1,0:T(8,128)} custom-call(f32[512,128]{1,0:T(8,128)S(1)} %bitcast.1, f32[4,512,128]{2,1,0:T(8,128)S(1)} %get-tuple-element.14.loc_ref, f32[1024,256]{1,0:T(8,128)S(1)} %get-tuple-element.15.q_ref, f32[1024,256]{1,0:T(8,128)S(1)} %get-tuple-element.16.img_ref, f32[4,2,256,256]{3,2,1,0:T(8,128)S(1)} %get-tuple-element.17.s_ref, ...), custom_call_target="tpu_custom_call" | custom-call | tf_op jit(solution)/shard_map/solve/pallas_call | solution.py:322

commit v3 on v2

v3 whole, which is shorter than its diff:
```python
import functools

import jax
import jax.numpy as jnp
from jax import lax
from jax.experimental import pallas as pl
from jax.experimental.pallas import tpu as pltpu
from jax.sharding import PartitionSpec as P

HEADS = 2
HEAD = 128
BLOCK = 256
ITERS = 4
ZDIM = 8
GROUP = 512
AHEAD = 3
F32 = jnp.float32
BF16 = jnp.bfloat16
MESH = pl.DeviceIdType.MESH


def halves(x):
    hi = x.astype(BF16)
    return hi, (x - hi.astype(F32)).astype(BF16)


def cat(*xs, axis):
    return jnp.concatenate(xs, axis=axis)


def mm(a, b):
    return jnp.dot(a, b, preferred_element_type=F32)


def mmt(a, b):
    return lax.dot_general(a, b, (((0,), (0,)), ((), ())), preferred_element_type=F32)


def narrow(a_hi, a_lo, b_hi, b_lo):
    right = cat(cat(b_hi, b_lo, axis=1), cat(b_hi, jnp.zeros_like(b_lo), axis=1), axis=0)
    t = mm(cat(a_hi, a_lo, axis=1), right)
    return t[:, :HEAD] + t[:, HEAD:]


def scores_of(a_hi, a_lo, kt_hi, kt_lo):
    return mm(cat(a_hi, a_lo, axis=1), cat(kt_hi, kt_hi, axis=0)) + mm(a_hi, kt_lo)


def weighted(s, b_hi, b_lo):
    s_hi, s_lo = halves(s)
    t = mm(s_hi, cat(b_hi, b_lo, axis=1))
    return t[:, :HEAD] + t[:, HEAD:] + mm(s_lo, b_hi)


def causal_mask():
    rows = lax.broadcasted_iota(jnp.int32, (BLOCK, BLOCK), 0)
    cols = lax.broadcasted_iota(jnp.int32, (BLOCK, BLOCK), 1)
    return cols <= rows


def lanes(h):
    return pl.ds(h * HEAD, HEAD)


def dots(a, b):
    return jnp.sum(a * b, axis=-1, keepdims=True)


def main_kernel(
    nz, q_hbm, k_hbm, v_hbm, x_ref, s_ref, vh_ref, state_ref,
    qbuf, kbuf, vbuf, img, kt, kh, near_a, near_b, near_s,
    sums, zin, zpre, xin, gin, eout, e,
    qsem, ksem, vsem, zs, zr, xs, xr, gs, gr, es, er,
):
    g, s = lax.axis_index("grp"), lax.axis_index("seq")
    ng, nx = lax.axis_size("grp"), lax.axis_size("seq") // nz
    z, x = s % nz, s // nz
    blocks = kbuf.shape[0] // BLOCK
    rows = HEADS * HEAD // nz

    def along_z(d):
        return {"grp": g, "seq": x * nz + (z + d) % nz}

    def along_x(d):
        return {"grp": g, "seq": ((x + d) % nx) * nz + z}

    def along_g(d):
        return {"grp": (g + d) % ng, "seq": s}

    def span(b):
        return pl.ds(b * BLOCK, BLOCK)

    k_loads = [pltpu.make_async_copy(k_hbm.at[span(b)], kbuf.at[span(b)], ksem.at[b]) for b in range(blocks)]
    v_loads = [pltpu.make_async_copy(v_hbm.at[span(b)], vbuf.at[span(b)], vsem.at[b]) for b in range(blocks)]
    q_load = pltpu.make_async_copy(q_hbm, qbuf, qsem)
    for load in k_loads + v_loads + [q_load]:
        load.start()
    barrier = pltpu.get_barrier_semaphore()
    partners = [along_z(d) for d in range(1, nz)] + [along_x(d) for d in range(1, nx)] + [along_g(d) for d in range(1, ng)]
    for partner in partners:
        pl.semaphore_signal(barrier, inc=1, device_id=partner, device_id_type=MESH)

    def remote(src, dst, send, recv, to):
        return pltpu.make_async_remote_copy(
            src_ref=src, dst_ref=dst, send_sem=send, recv_sem=recv, device_id=to, device_id_type=MESH)

    def zcopy(c, d):
        return remote(sums.at[c, (z + d) % nz], zin.at[c, z], zs.at[c, d], zr.at[c, d], along_z(d))

    def xcopy(c, d):
        return remote(xin.at[c, x], xin.at[c, x], xs.at[c, d], xr.at[c, d], along_x(d))

    def gcopy(c, d):
        return remote(gin.at[c, g], gin.at[c, g], gs.at[c, d], gr.at[c, d], along_g(d))

    def ecopy(c, d):
        return remote(eout.at[c, (z + d) % nz], e.at[c, z], es.at[c, d], er.at[c, d], along_z(d))

    far_first = sorted(range(1, nz), key=lambda d: -min(d, nz - d))
    half = nz // HEADS

    def send_sums(c, parts):
        for h, part in enumerate(parts):
            sums[c, pl.ds(h * half, half)] = part.reshape(half, rows, HEAD)
        for d in far_first:
            zcopy(c, d).start()
        zin[c, z] = sums[c, z]

    total_a = [jnp.zeros((HEAD, HEAD), F32) for _ in range(HEADS)]
    total_b = [jnp.zeros((HEAD, HEAD), F32) for _ in range(HEADS)]
    for b in range(blocks):
        k_loads[b].wait()
        for h in range(HEADS):
            k_hi, k_lo = halves(kbuf[span(b), lanes(h)])
            kh[0, b, h] = k_hi
            kh[1, b, h] = k_lo
            wide = mmt(k_hi, cat(k_hi, k_lo, axis=1))
            near_a[b, h] = total_a[h]
            near_b[b, h] = total_b[h]
            total_a[h] = total_a[h] + (wide[:, :HEAD] + wide[:, HEAD:])
            total_b[h] = total_b[h] + wide[:, HEAD:]
    grams = [total_a[h] + total_b[h].T for h in range(HEADS)]
    pl.semaphore_wait(barrier, len(partners))
    send_sums(0, grams)

    total_s = [jnp.zeros((HEAD, HEAD), F32) for _ in range(HEADS)]
    for b in range(blocks):
        v_loads[b].wait()
        for h in range(HEADS):
            v_hi, v_lo = halves(vbuf[span(b), lanes(h)])
            vh_ref[0, b, h] = v_hi
            vh_ref[1, b, h] = v_lo
            wide = mmt(kh[0, b, h], cat(v_hi, v_lo, axis=1))
            near_s[b, h] = total_s[h]
            total_s[h] = total_s[h] + (wide[:, :HEAD] + wide[:, HEAD:] + mmt(kh[1, b, h], v_hi))
    send_sums(1, total_s)

    q_load.wait()

    def local_part(b):
        causal = causal_mask()
        row = pl.ds(pl.multiple_of(b * BLOCK, BLOCK), BLOCK)
        for h in range(HEADS):
            q = qbuf[row, lanes(h)]
            q_hi, q_lo = halves(q)
            kt_hi, kt_lo = halves(kbuf[row, lanes(h)].T)
            kt[0, b, h] = kt_hi
            kt[1, b, h] = kt_lo
            scores = jnp.where(causal, scores_of(q_hi, q_lo, kt_hi, kt_lo), 0.0)
            s_ref[b, h] = scores
            gram = near_a[b, h] + near_b[b, h].T
            near_a[b, h] = gram
            near = weighted(scores, kh[0, b, h], kh[1, b, h])
            img[row, lanes(h)] = near + narrow(q_hi, q_lo, *halves(gram)) + q

    pl.loop(0, AHEAD)(local_part)

    zero = jnp.zeros((rows, HEAD), F32)
    held = {}

    def after_z(c):
        for d in range(1, nz):
            zcopy(c, d).wait_recv()
        run = zero
        for j in range(nz):
            zpre[c, j] = run
            run = run + zin[c, j]
        xin[c, x] = run
        for d in range(1, nx):
            xcopy(c, d).start()

    def after_x(c):
        for d in range(1, nx):
            xcopy(c, d).wait_recv()
        before, whole = zero, zero
        for j in range(nx):
            piece = xin[c, j]
            before = before + jnp.where(j < x, piece, 0.0)
            whole = whole + piece
        held[c] = before
        gin[c, g] = whole
        for d in range(1, ng):
            @pl.when(g + d < ng)
            def _():
                gcopy(c, d).start()

    def after_g(c):
        for d in range(1, ng):
            @pl.when(g - d >= 0)
            def _():
                gcopy(c, d).wait_recv()
        before = held[c] + lax.fori_loop(0, g, lambda j, acc: acc + gin[c, j], zero)
        for j in range(nz):
            eout[c, j] = zpre[c, j] + before
        for d in far_first:
            ecopy(c, d).start()
        e[c, z] = eout[c, z]

    for c in range(2):
        after_z(c)
    for c in range(2):
        after_x(c)
    for c in range(2):
        after_g(c)
    pl.loop(AHEAD, blocks)(local_part)
    for d in range(1, nz):
        ecopy(0, d).wait_recv()

    @pl.loop(0, blocks * BLOCK // GROUP)
    def _(i):
        causal = causal_mask()
        work = []
        for c in range(GROUP // BLOCK):
            for h in range(HEADS):
                n = i * (GROUP // BLOCK) + c
                row = pl.ds(pl.multiple_of(n * BLOCK, BLOCK), BLOCK)
                enter = e[0, pl.ds(h * half, half)].reshape(HEAD, HEAD)
                q = qbuf[row, lanes(h)]
                work.append(dict(
                    n=n, h=h, row=row, enter=halves(enter), gram=halves(enter + near_a[n, h]),
                    x=None, r=q, p=q, rr=dots(q, q), acc=None))
        for step in range(ITERS):
            images, scores = [], []
            for st in work:
                n, h = st["n"], st["h"]
                p_hi, p_lo = halves(st["p"])
                if step == 0:
                    scores.append(s_ref[n, h])
                    images.append(narrow(p_hi, p_lo, *st["enter"]) + img[st["row"], lanes(h)])
                else:
                    sc = jnp.where(causal, scores_of(p_hi, p_lo, kt[0, n, h], kt[1, n, h]), 0.0)
                    scores.append(sc)
                    images.append(narrow(p_hi, p_lo, *st["gram"]) + weighted(sc, kh[0, n, h], kh[1, n, h]) + st["p"])
            for st, image, sc in zip(work, images, scores):
                alpha = st["rr"] / dots(st["p"], image)
                st["x"] = alpha * st["p"] if step == 0 else st["x"] + alpha * st["p"]
                st["acc"] = alpha * sc if step == 0 else st["acc"] + alpha * sc
                if step < ITERS - 1:
                    st["r"] = st["r"] - alpha * image
                    new = dots(st["r"], st["r"])
                    st["p"] = st["r"] + new / st["rr"] * st["p"]
                    st["rr"] = new
        for st in work:
            x_ref[st["row"], lanes(st["h"])] = st["x"]
            s_ref[st["n"], st["h"]] = st["acc"]

    for d in range(1, nz):
        ecopy(1, d).wait_recv()
    for h in range(HEADS):
        for b in range(blocks):
            hi, lo = halves(e[1, pl.ds(h * half, half)].reshape(HEAD, HEAD) + near_s[b, h])
            state_ref[0, b, h] = hi
            state_ref[1, b, h] = lo
    for c in range(2):
        for d in range(1, nz):
            zcopy(c, d).wait_send()
            ecopy(c, d).wait_send()
        for d in range(1, nx):
            xcopy(c, d).wait_send()
        for d in range(1, ng):
            @pl.when(g + d < ng)
            def _():
                gcopy(c, d).wait_send()


def steps(queries, keys, values, nz):
    tokens, width = keys.shape
    blocks = tokens // BLOCK
    nx, ng = lax.axis_size("seq") // nz, lax.axis_size("grp")
    rows = HEADS * HEAD // nz
    hbm = pl.BlockSpec(memory_space=pltpu.HBM)
    vmem = pl.BlockSpec(memory_space=pltpu.VMEM)
    dma = pltpu.SemaphoreType.DMA
    outs = (
        pltpu.VMEM((tokens, width), F32),
        pltpu.VMEM((blocks, HEADS, BLOCK, BLOCK), F32),
        pltpu.VMEM((2, blocks, HEADS, BLOCK, HEAD), BF16),
        pltpu.VMEM((2, blocks, HEADS, HEAD, HEAD), BF16),
    )
    square = pltpu.VMEM((blocks, HEADS, HEAD, HEAD), F32)
    pieces = pltpu.VMEM((2, nz, rows, HEAD), F32)
    return pl.pallas_call(
        functools.partial(main_kernel, nz),
        out_shape=outs,
        in_specs=[hbm] * 3,
        out_specs=(vmem,) * len(outs),
        scratch_shapes=[
            pltpu.VMEM((tokens, width), F32),
            pltpu.VMEM((tokens, width), F32),
            pltpu.VMEM((tokens, width), F32),
            pltpu.VMEM((tokens, width), F32),
            pltpu.VMEM((2, blocks, HEADS, HEAD, BLOCK), BF16),
            pltpu.VMEM((2, blocks, HEADS, BLOCK, HEAD), BF16),
            square, square, square,
            pieces, pieces, pieces,
            pltpu.VMEM((2, nx, rows, HEAD), F32),
            pltpu.VMEM((2, ng, rows, HEAD), F32),
            pieces, pieces,
            dma, dma((blocks,)), dma((blocks,)),
            dma((2, nz)), dma((2, nz)), dma((2, nx)), dma((2, nx)),
            dma((2, ng)), dma((2, ng)), dma((2, nz)), dma((2, nz)),
        ],
        compiler_params=pltpu.CompilerParams(collective_id=0, has_side_effects=True, vmem_limit_bytes=61_600_000),
        name="steps",
    )(queries, keys, values)


def last_kernel(x_ref, s_ref, vh_ref, state_ref, out_ref):
    first = lax.axis_index("grp") * lax.axis_size("seq") + lax.axis_index("seq")
    first = (first * pl.num_programs(0) + pl.program_id(0)) * BLOCK
    scale = jnp.sqrt((first + lax.broadcasted_iota(jnp.int32, (BLOCK, HEAD), 0)).astype(F32) + 1.0)
    n = pl.program_id(0)
    row = pl.ds(pl.multiple_of(n * BLOCK, BLOCK), BLOCK)
    for h in range(HEADS):
        out = narrow(*halves(x_ref[row, lanes(h)]), state_ref[0, n, h], state_ref[1, n, h])
        out = out + weighted(s_ref[n, h], vh_ref[0, n, h], vh_ref[1, n, h])
        out_ref[:, lanes(h)] = out * scale


def last(*parts):
    tokens, width = parts[0].shape
    return pl.pallas_call(
        last_kernel,
        grid=(tokens // BLOCK,),
        out_shape=jax.ShapeDtypeStruct((tokens, width), F32),
        in_specs=[pl.BlockSpec(memory_space=pltpu.VMEM)] * len(parts),
        out_specs=pl.BlockSpec((BLOCK, width), lambda n: (n, 0)),
        compiler_params=pltpu.CompilerParams(vmem_limit_bytes=16 * 2**20),
        name="last",
    )(*parts)


def on_device(queries, keys, values):
    return last(*steps(queries, keys, values, ZDIM))


def solution(mesh):
    return jax.shard_map(
        on_device,
        mesh=mesh,
        in_specs=(P(("grp", "seq"), None), P(("grp", "seq"), None), P(("grp", "seq"), None)),
        out_specs=P(("grp", "seq"), None),
        check_vma=False,
    )
```

time: 41.1 us -> 40.2 us (0.978)
  Pallas kernels: 40.9 us -> 40.1 us
    pallas_call x2, Pallas kernels: 40.9 us -> 40.1 us  [the longest x1 37.5 us: steps(): pl.pallas_call(functools.partial(main_kernel, nz), out_shape=outs, in_spe...]
where the time goes in v3:
time: 40.2 us; the launch traced here: 40.1 us
  Pallas kernels  40.1 us (100%)
    pallas_call x1, Pallas kernels, steps(): pl.pallas_call(functools.partial(main_kernel, nz), out_shape=outs, in_spe...  37.5 us
    pallas_call x1, Pallas kernels, last(): pl.pallas_call(last_kernel, grid=(tokens // BLOCK,), out_shape=jax.ShapeD...  2.59 us

profile of v3, /device:TPU:24, one launch (start us, length us, event | category | flops | bytes accessed | tf_op | source)
XLA Modules:
  0.0 40.1 jit_solution(10760668597539729909)
XLA Ops:
  0.0 37.5 %steps.1 = (f32[1024,256]{1,0:T(8,128)S(1)}, f32[4,2,256,256]{3,2,1,0:T(8,128)S(1)}, bf16[2,4,2,256,128]{4,3,2,1,0:T(8,128)(2,1)S(1)}, bf16[2,4,2,128,128]{4,3,2,1,0:T(8,128)(2,1)S(1)}) custom-call(f32[1024,256]{1,0:T(8,128)} %q_hbm.1, f32[1024,256]{1,0:T(8,128)} %k_hbm.1, f32[1024,256]{1,0:T(8,128)} %v_hbm.1), custom_call_target="tpu_custom_call" | custom-call | tf_op jit(solution)/shard_map/steps/pallas_call | solution.py:302
  37.5 2.6 %last.1 = f32[1024,256]{1,0:T(8,128)} custom-call(f32[1024,256]{1,0:T(8,128)S(1)} %get-tuple-element.9.x_ref, f32[4,2,256,256]{3,2,1,0:T(8,128)S(1)} %get-tuple-element.10.s_ref, bf16[2,4,2,256,128]{4,3,2,1,0:T(8,128)(2,1)S(1)} %get-tuple-element.11.vh_ref, bf16[2,4,2,128,128]{4,3,2,1,0:T(8,128)(2,1)S(1)} %get-tuple-element.12.state_ref), custom_call_target="tpu_custom_call" | custom-call | tf_op jit(solution)/shard_map/last/pallas_call | solution.py:342

commit v4 on v3

--- a/solution.py
+++ b/solution.py
@@ -12,7 +12,7 @@
 BLOCK = 256
 ITERS = 4
 ZDIM = 8
-GROUP = 512
+GROUP = 1024
 AHEAD = 3
 F32 = jnp.float32
 BF16 = jnp.bfloat16
@@ -43,13 +43,14 @@
 
 
 def scores_of(a_hi, a_lo, kt_hi, kt_lo):
-    return mm(cat(a_hi, a_lo, axis=1), cat(kt_hi, kt_hi, axis=0)) + mm(a_hi, kt_lo)
+    t = mm(cat(a_hi, a_lo, axis=0), kt_hi)
+    return t[:BLOCK] + t[BLOCK:] + mm(a_hi, kt_lo)
 
 
 def weighted(s, b_hi, b_lo):
     s_hi, s_lo = halves(s)
-    t = mm(s_hi, cat(b_hi, b_lo, axis=1))
-    return t[:, :HEAD] + t[:, HEAD:] + mm(s_lo, b_hi)
+    t = mm(cat(s_hi, s_lo, axis=0), cat(b_hi, b_lo, axis=1))
+    return t[:BLOCK, :HEAD] + t[:BLOCK, HEAD:] + t[BLOCK:, :HEAD]
 
 
 def causal_mask():
@@ -67,8 +68,8 @@
 
 
 def main_kernel(
-    nz, q_hbm, k_hbm, v_hbm, x_ref, s_ref, vh_ref, state_ref,
-    qbuf, kbuf, vbuf, img, kt, kh, near_a, near_b, near_s,
+    nz, q_hbm, k_hbm, v_hbm, x_ref, near_ref, state_ref,
+    qbuf, kbuf, vbuf, img, s_ref, kt, kh, vh, near_a, near_b, near_s,
     sums, zin, zpre, xin, gin, eout, e,
     qsem, ksem, vsem, zs, zr, xs, xr, gs, gr, es, er,
 ):
@@ -93,7 +94,7 @@
     k_loads = [pltpu.make_async_copy(k_hbm.at[span(b)], kbuf.at[span(b)], ksem.at[b]) for b in range(blocks)]
     v_loads = [pltpu.make_async_copy(v_hbm.at[span(b)], vbuf.at[span(b)], vsem.at[b]) for b in range(blocks)]
     q_load = pltpu.make_async_copy(q_hbm, qbuf, qsem)
-    for load in k_loads + v_loads + [q_load]:
+    for load in k_loads:
         load.start()
     barrier = pltpu.get_barrier_semaphore()
     partners = [along_z(d) for d in range(1, nz)] + [along_x(d) for d in range(1, nx)] + [along_g(d) for d in range(1, ng)]
@@ -119,9 +120,11 @@
     far_first = sorted(range(1, nz), key=lambda d: -min(d, nz - d))
     half = nz // HEADS
 
-    def send_sums(c, parts):
+    def keep_sums(c, parts):
         for h, part in enumerate(parts):
             sums[c, pl.ds(h * half, half)] = part.reshape(half, rows, HEAD)
+
+    def send_sums(c):
         for d in far_first:
             zcopy(c, d).start()
         zin[c, z] = sums[c, z]
@@ -130,6 +133,9 @@
     total_b = [jnp.zeros((HEAD, HEAD), F32) for _ in range(HEADS)]
     for b in range(blocks):
         k_loads[b].wait()
+        if b == blocks - 1:
+            for load in v_loads + [q_load]:
+                load.start()
         for h in range(HEADS):
             k_hi, k_lo = halves(kbuf[span(b), lanes(h)])
             kh[0, b, h] = k_hi
@@ -141,19 +147,20 @@
             total_b[h] = total_b[h] + wide[:, HEAD:]
     grams = [total_a[h] + total_b[h].T for h in range(HEADS)]
     pl.semaphore_wait(barrier, len(partners))
-    send_sums(0, grams)
+    keep_sums(0, grams)
+    send_sums(0)
 
     total_s = [jnp.zeros((HEAD, HEAD), F32) for _ in range(HEADS)]
     for b in range(blocks):
         v_loads[b].wait()
         for h in range(HEADS):
             v_hi, v_lo = halves(vbuf[span(b), lanes(h)])
-            vh_ref[0, b, h] = v_hi
-            vh_ref[1, b, h] = v_lo
+            vh[0, b, h] = v_hi
+            vh[1, b, h] = v_lo
             wide = mmt(kh[0, b, h], cat(v_hi, v_lo, axis=1))
             near_s[b, h] = total_s[h]
             total_s[h] = total_s[h] + (wide[:, :HEAD] + wide[:, HEAD:] + mmt(kh[1, b, h], v_hi))
-    send_sums(1, total_s)
+    keep_sums(1, total_s)
 
     q_load.wait()
 
@@ -216,18 +223,7 @@
             ecopy(c, d).start()
         e[c, z] = eout[c, z]
 
-    for c in range(2):
-        after_z(c)
-    for c in range(2):
-        after_x(c)
-    for c in range(2):
-        after_g(c)
-    pl.loop(AHEAD, blocks)(local_part)
-    for d in range(1, nz):
-        ecopy(0, d).wait_recv()
-
-    @pl.loop(0, blocks * BLOCK // GROUP)
-    def _(i):
+    def solve_group(i):
         causal = causal_mask()
         work = []
         for c in range(GROUP // BLOCK):
@@ -261,9 +257,22 @@
                     st["p"] = st["r"] + new / st["rr"] * st["p"]
                     st["rr"] = new
         for st in work:
-            x_ref[st["row"], lanes(st["h"])] = st["x"]
-            s_ref[st["n"], st["h"]] = st["acc"]
-
+            n, h = st["n"], st["h"]
+            x_ref[st["row"], lanes(h)] = st["x"]
+            near_ref[st["row"], lanes(h)] = weighted(st["acc"], vh[0, n, h], vh[1, n, h])
+
+    groups = blocks * BLOCK // GROUP
+    after_z(0)
+    send_sums(1)
+    after_x(0)
+    after_z(1)
+    after_g(0)
+    after_x(1)
+    pl.loop(AHEAD, blocks)(local_part)
+    after_g(1)
+    for d in range(1, nz):
+        ecopy(0, d).wait_recv()
+    pl.loop(0, groups)(solve_group)
     for d in range(1, nz):
         ecopy(1, d).wait_recv()
     for h in range(HEADS):
@@ -293,8 +302,7 @@
     dma = pltpu.SemaphoreType.DMA
     outs = (
         pltpu.VMEM((tokens, width), F32),
-        pltpu.VMEM((blocks, HEADS, BLOCK, BLOCK), F32),
-        pltpu.VMEM((2, blocks, HEADS, BLOCK, HEAD), BF16),
+        pltpu.VMEM((tokens, width), F32),
         pltpu.VMEM((2, blocks, HEADS, HEAD, HEAD), BF16),
     )
     square = pltpu.VMEM((blocks, HEADS, HEAD, HEAD), F32)
@@ -309,7 +317,9 @@
             pltpu.VMEM((tokens, width), F32),
             pltpu.VMEM((tokens, width), F32),
             pltpu.VMEM((tokens, width), F32),
+            pltpu.VMEM((blocks, HEADS, BLOCK, BLOCK), F32),
             pltpu.VMEM((2, blocks, HEADS, HEAD, BLOCK), BF16),
+            pltpu.VMEM((2, blocks, HEADS, BLOCK, HEAD), BF16),
             pltpu.VMEM((2, blocks, HEADS, BLOCK, HEAD), BF16),
             square, square, square,
             pieces, pieces, pieces,
@@ -320,31 +330,32 @@
             dma((2, nz)), dma((2, nz)), dma((2, nx)), dma((2, nx)),
             dma((2, ng)), dma((2, ng)), dma((2, nz)), dma((2, nz)),
         ],
-        compiler_params=pltpu.CompilerParams(collective_id=0, has_side_effects=True, vmem_limit_bytes=61_600_000),
+        compiler_params=pltpu.CompilerParams(collective_id=0, has_side_effects=True, vmem_limit_bytes=63_400_000),
         name="steps",
     )(queries, keys, values)
 
 
-def last_kernel(x_ref, s_ref, vh_ref, state_ref, out_ref):
+def last_kernel(x_ref, near_ref, state_ref, out_ref):
     first = lax.axis_index("grp") * lax.axis_size("seq") + lax.axis_index("seq")
-    first = (first * pl.num_programs(0) + pl.program_id(0)) * BLOCK
-    scale = jnp.sqrt((first + lax.broadcasted_iota(jnp.int32, (BLOCK, HEAD), 0)).astype(F32) + 1.0)
-    n = pl.program_id(0)
-    row = pl.ds(pl.multiple_of(n * BLOCK, BLOCK), BLOCK)
-    for h in range(HEADS):
-        out = narrow(*halves(x_ref[row, lanes(h)]), state_ref[0, n, h], state_ref[1, n, h])
-        out = out + weighted(s_ref[n, h], vh_ref[0, n, h], vh_ref[1, n, h])
-        out_ref[:, lanes(h)] = out * scale
+    first = (first * pl.num_programs(0) + pl.program_id(0)) * GROUP
+    for c in range(GROUP // BLOCK):
+        n = pl.program_id(0) * (GROUP // BLOCK) + c
+        row = pl.ds(pl.multiple_of(n * BLOCK, BLOCK), BLOCK)
+        place = (first + c * BLOCK + lax.broadcasted_iota(jnp.int32, (BLOCK, HEAD), 0)).astype(F32)
+        scale = jnp.sqrt(place + 1.0)
+        for h in range(HEADS):
+            out = narrow(*halves(x_ref[row, lanes(h)]), state_ref[0, n, h], state_ref[1, n, h])
+            out_ref[pl.ds(c * BLOCK, BLOCK), lanes(h)] = (out + near_ref[row, lanes(h)]) * scale
 
 
 def last(*parts):
     tokens, width = parts[0].shape
     return pl.pallas_call(
         last_kernel,
-        grid=(tokens // BLOCK,),
+        grid=(tokens // GROUP,),
         out_shape=jax.ShapeDtypeStruct((tokens, width), F32),
         in_specs=[pl.BlockSpec(memory_space=pltpu.VMEM)] * len(parts),
-        out_specs=pl.BlockSpec((BLOCK, width), lambda n: (n, 0)),
+        out_specs=pl.BlockSpec((GROUP, width), lambda n: (n, 0)),
         compiler_params=pltpu.CompilerParams(vmem_limit_bytes=16 * 2**20),
         name="last",
     )(*parts)

time: 40.2 us -> 35.5 us (0.88)
  Pallas kernels: 40.1 us -> 35.4 us
    pallas_call x1, Pallas kernels: 37.5 us -> 33.9 us  [steps(): pl.pallas_call(functools.partial(main_kernel, nz), out_shape=outs, in_spe...]
    pallas_call x1, Pallas kernels: 2.59 us -> 1.45 us  [last(): pl.pallas_call(last_kernel, grid=(tokens // GROUP,), out_shape=jax.ShapeD...]
where the time goes in v4:
time: 35.5 us; the launch traced here: 35.4 us
  Pallas kernels  35.4 us (100%)
    pallas_call x1, Pallas kernels, steps(): pl.pallas_call(functools.partial(main_kernel, nz), out_shape=outs, in_spe...  33.9 us
    pallas_call x1, Pallas kernels, last(): pl.pallas_call(last_kernel, grid=(tokens // GROUP,), out_shape=jax.ShapeD...  1.45 us

profile of v4, /device:TPU:24, one launch (start us, length us, event | category | flops | bytes accessed | tf_op | source)
XLA Modules:
  0.0 35.4 jit_solution(1831491929458748693)
XLA Ops:
  0.0 33.9 %steps.1 = (f32[1024,256]{1,0:T(8,128)S(1)}, f32[1024,256]{1,0:T(8,128)S(1)}, bf16[2,4,2,128,128]{4,3,2,1,0:T(8,128)(2,1)S(1)}) custom-call(f32[1024,256]{1,0:T(8,128)} %q_hbm.1, f32[1024,256]{1,0:T(8,128)} %k_hbm.1, f32[1024,256]{1,0:T(8,128)} %v_hbm.1), custom_call_target="tpu_custom_call" | custom-call | tf_op jit(solution)/shard_map/steps/pallas_call | solution.py:310
  33.9 1.5 %last.1 = f32[1024,256]{1,0:T(8,128)} custom-call(f32[1024,256]{1,0:T(8,128)S(1)} %get-tuple-element.8.x_ref, f32[1024,256]{1,0:T(8,128)S(1)} %get-tuple-element.9.near_ref, bf16[2,4,2,128,128]{4,3,2,1,0:T(8,128)(2,1)S(1)} %get-tuple-element.10.state_ref), custom_call_target="tpu_custom_call" | custom-call | tf_op jit(solution)/shard_map/last/pallas_call | solution.py:353

commit v5 on v4

--- a/solution.py
+++ b/solution.py
@@ -67,26 +67,18 @@
     return jnp.sum(a * b, axis=-1, keepdims=True)
 
 
+def energy(a, b):
+    return jnp.sum(a + (b[:, :HEAD] + b[:, HEAD:]), axis=-1, keepdims=True)
+
+
 def main_kernel(
     nz, q_hbm, k_hbm, v_hbm, x_ref, near_ref, state_ref,
     qbuf, kbuf, vbuf, img, s_ref, kt, kh, vh, near_a, near_b, near_s,
     sums, zin, zpre, xin, gin, eout, e,
     qsem, ksem, vsem, zs, zr, xs, xr, gs, gr, es, er,
 ):
-    g, s = lax.axis_index("grp"), lax.axis_index("seq")
-    ng, nx = lax.axis_size("grp"), lax.axis_size("seq") // nz
-    z, x = s % nz, s // nz
     blocks = kbuf.shape[0] // BLOCK
     rows = HEADS * HEAD // nz
-
-    def along_z(d):
-        return {"grp": g, "seq": x * nz + (z + d) % nz}
-
-    def along_x(d):
-        return {"grp": g, "seq": ((x + d) % nx) * nz + z}
-
-    def along_g(d):
-        return {"grp": (g + d) % ng, "seq": s}
 
     def span(b):
         return pl.ds(b * BLOCK, BLOCK)
@@ -96,6 +88,19 @@
     q_load = pltpu.make_async_copy(q_hbm, qbuf, qsem)
     for load in k_loads:
         load.start()
+    g, s = lax.axis_index("grp"), lax.axis_index("seq")
+    ng, nx = lax.axis_size("grp"), lax.axis_size("seq") // nz
+    z, x = s % nz, s // nz
+
+    def along_z(d):
+        return {"grp": g, "seq": x * nz + (z + d) % nz}
+
+    def along_x(d):
+        return {"grp": g, "seq": ((x + d) % nx) * nz + z}
+
+    def along_g(d):
+        return {"grp": (g + d) % ng, "seq": s}
+
     barrier = pltpu.get_barrier_semaphore()
     partners = [along_z(d) for d in range(1, nz)] + [along_x(d) for d in range(1, nx)] + [along_g(d) for d in range(1, ng)]
     for partner in partners:
@@ -219,8 +224,8 @@
         before = held[c] + lax.fori_loop(0, g, lambda j, acc: acc + gin[c, j], zero)
         for j in range(nz):
             eout[c, j] = zpre[c, j] + before
-        for d in far_first:
-            ecopy(c, d).start()
+        for i in range(nz - 1):
+            ecopy(c, (i + (i >= z).astype(jnp.int32) - z + nz) % nz).start()
         e[c, z] = eout[c, z]
 
     def solve_group(i):
@@ -246,9 +251,13 @@
                 else:
                     sc = jnp.where(causal, scores_of(p_hi, p_lo, kt[0, n, h], kt[1, n, h]), 0.0)
                     scores.append(sc)
-                    images.append(narrow(p_hi, p_lo, *st["gram"]) + weighted(sc, kh[0, n, h], kh[1, n, h]) + st["p"])
+                    image = narrow(p_hi, p_lo, *st["gram"]) + st["p"]
+                    images.append(image if step == ITERS - 1 else image + weighted(sc, kh[0, n, h], kh[1, n, h]))
             for st, image, sc in zip(work, images, scores):
-                alpha = st["rr"] / dots(st["p"], image)
+                if step == ITERS - 1:
+                    alpha = st["rr"] / energy(st["p"] * image, sc * sc)
+                else:
+                    alpha = st["rr"] / dots(st["p"], image)
                 st["x"] = alpha * st["p"] if step == 0 else st["x"] + alpha * st["p"]
                 st["acc"] = alpha * sc if step == 0 else st["acc"] + alpha * sc
                 if step < ITERS - 1:

time: 35.5 us -> 34.8 us (0.980)
  Pallas kernels: 35.4 us -> 34.4 us
    pallas_call x1, Pallas kernels: 33.9 us -> 32.9 us  [steps(): pl.pallas_call(functools.partial(main_kernel, nz), out_shape=outs, in_spe...]
where the time goes in v5:
time: 34.8 us; the launch traced here: 34.4 us
  Pallas kernels  34.4 us (99%)
    pallas_call x1, Pallas kernels, steps(): pl.pallas_call(functools.partial(main_kernel, nz), out_shape=outs, in_spe...  32.9 us
    pallas_call x1, Pallas kernels, last(): pl.pallas_call(last_kernel, grid=(tokens // GROUP,), out_shape=jax.ShapeD...  1.45 us

profile of v5, /device:TPU:24, one launch (start us, length us, event | category | flops | bytes accessed | tf_op | source)
XLA Modules:
  0.0 34.4 jit_solution(12222433718375476227)
XLA Ops:
  0.0 32.9 %steps.1 = (f32[1024,256]{1,0:T(8,128)S(1)}, f32[1024,256]{1,0:T(8,128)S(1)}, bf16[2,4,2,128,128]{4,3,2,1,0:T(8,128)(2,1)S(1)}) custom-call(f32[1024,256]{1,0:T(8,128)} %q_hbm.1, f32[1024,256]{1,0:T(8,128)} %k_hbm.1, f32[1024,256]{1,0:T(8,128)} %v_hbm.1), custom_call_target="tpu_custom_call" | custom-call | tf_op jit(solution)/shard_map/steps/pallas_call | solution.py:319
  32.9 1.5 %last.1 = f32[1024,256]{1,0:T(8,128)} custom-call(f32[1024,256]{1,0:T(8,128)S(1)} %get-tuple-element.8.x_ref, f32[1024,256]{1,0:T(8,128)S(1)} %get-tuple-element.9.near_ref, bf16[2,4,2,128,128]{4,3,2,1,0:T(8,128)(2,1)S(1)} %get-tuple-element.10.state_ref), custom_call_target="tpu_custom_call" | custom-call | tf_op jit(solution)/shard_map/last/pallas_call | solution.py:362

commit v6 on v5

--- a/solution.py
+++ b/solution.py
@@ -13,7 +13,7 @@
 ITERS = 4
 ZDIM = 8
 GROUP = 1024
-AHEAD = 3
+AHEAD = 2
 F32 = jnp.float32
 BF16 = jnp.bfloat16
 MESH = pl.DeviceIdType.MESH
@@ -43,8 +43,7 @@
 
 
 def scores_of(a_hi, a_lo, kt_hi, kt_lo):
-    t = mm(cat(a_hi, a_lo, axis=0), kt_hi)
-    return t[:BLOCK] + t[BLOCK:] + mm(a_hi, kt_lo)
+    return mm(cat(a_hi, a_lo, axis=1), cat(kt_hi, kt_hi, axis=0)) + mm(a_hi, kt_lo)
 
 
 def weighted(s, b_hi, b_lo):
@@ -72,8 +71,8 @@
 
 
 def main_kernel(
-    nz, q_hbm, k_hbm, v_hbm, x_ref, near_ref, state_ref,
-    qbuf, kbuf, vbuf, img, s_ref, kt, kh, vh, near_a, near_b, near_s,
+    nz, q_hbm, k_hbm, v_hbm, x_ref, near_ref, state_ref, near_s,
+    qbuf, kbuf, vbuf, img, s_ref, kt, kh, vh, near_a, near_b,
     sums, zin, zpre, xin, gin, eout, e,
     qsem, ksem, vsem, zs, zr, xs, xr, gs, gr, es, er,
 ):
@@ -110,6 +109,9 @@
         return pltpu.make_async_remote_copy(
             src_ref=src, dst_ref=dst, send_sem=send, recv_sem=recv, device_id=to, device_id_type=MESH)
 
+    def landing(c):
+        return state_ref if c else e
+
     def zcopy(c, d):
         return remote(sums.at[c, (z + d) % nz], zin.at[c, z], zs.at[c, d], zr.at[c, d], along_z(d))
 
@@ -120,7 +122,7 @@
         return remote(gin.at[c, g], gin.at[c, g], gs.at[c, d], gr.at[c, d], along_g(d))
 
     def ecopy(c, d):
-        return remote(eout.at[c, (z + d) % nz], e.at[c, z], es.at[c, d], er.at[c, d], along_z(d))
+        return remote(eout.at[c, (z + d) % nz], landing(c).at[z], es.at[c, d], er.at[c, d], along_z(d))
 
     far_first = sorted(range(1, nz), key=lambda d: -min(d, nz - d))
     half = nz // HEADS
@@ -179,7 +181,7 @@
             kt[0, b, h] = kt_hi
             kt[1, b, h] = kt_lo
             scores = jnp.where(causal, scores_of(q_hi, q_lo, kt_hi, kt_lo), 0.0)
-            s_ref[b, h] = scores
+            s_ref[0, b, h] = scores
             gram = near_a[b, h] + near_b[b, h].T
             near_a[b, h] = gram
             near = weighted(scores, kh[0, b, h], kh[1, b, h])
@@ -226,53 +228,63 @@
             eout[c, j] = zpre[c, j] + before
         for i in range(nz - 1):
             ecopy(c, (i + (i >= z).astype(jnp.int32) - z + nz) % nz).start()
-        e[c, z] = eout[c, z]
+        landing(c)[z] = eout[c, z]
 
     def solve_group(i):
         causal = causal_mask()
         work = []
+        every = pl.ds(pl.multiple_of(i * GROUP, GROUP), GROUP)
+        enter = [e[pl.ds(h * half, half)].reshape(HEAD, HEAD) for h in range(HEADS)]
+        far = [narrow(*halves(qbuf[every, lanes(h)]), *halves(enter[h])) for h in range(HEADS)]
         for c in range(GROUP // BLOCK):
             for h in range(HEADS):
                 n = i * (GROUP // BLOCK) + c
                 row = pl.ds(pl.multiple_of(n * BLOCK, BLOCK), BLOCK)
-                enter = e[0, pl.ds(h * half, half)].reshape(HEAD, HEAD)
                 q = qbuf[row, lanes(h)]
                 work.append(dict(
-                    n=n, h=h, row=row, enter=halves(enter), gram=halves(enter + near_a[n, h]),
-                    x=None, r=q, p=q, rr=dots(q, q), acc=None))
-        for step in range(ITERS):
+                    n=n, h=h, row=row, far=far[h][c * BLOCK : (c + 1) * BLOCK], gram=halves(enter[h] + near_a[n, h]),
+                    r=q, p=q, rr=dots(q, q)))
+        for step in range(ITERS - 1):
             images, scores = [], []
             for st in work:
                 n, h = st["n"], st["h"]
-                p_hi, p_lo = halves(st["p"])
                 if step == 0:
-                    scores.append(s_ref[n, h])
-                    images.append(narrow(p_hi, p_lo, *st["enter"]) + img[st["row"], lanes(h)])
+                    scores.append(s_ref[0, n, h])
+                    images.append(st["far"] + img[st["row"], lanes(h)])
                 else:
+                    p_hi, p_lo = halves(st["p"])
                     sc = jnp.where(causal, scores_of(p_hi, p_lo, kt[0, n, h], kt[1, n, h]), 0.0)
                     scores.append(sc)
-                    image = narrow(p_hi, p_lo, *st["gram"]) + st["p"]
-                    images.append(image if step == ITERS - 1 else image + weighted(sc, kh[0, n, h], kh[1, n, h]))
+                    images.append(narrow(p_hi, p_lo, *st["gram"]) + weighted(sc, kh[0, n, h], kh[1, n, h]) + st["p"])
             for st, image, sc in zip(work, images, scores):
-                if step == ITERS - 1:
-                    alpha = st["rr"] / energy(st["p"] * image, sc * sc)
-                else:
-                    alpha = st["rr"] / dots(st["p"], image)
+                alpha = st["rr"] / dots(st["p"], image)
+                st["acc"] = alpha * sc if step == 0 else st["acc"] + alpha * sc
                 st["x"] = alpha * st["p"] if step == 0 else st["x"] + alpha * st["p"]
-                st["acc"] = alpha * sc if step == 0 else st["acc"] + alpha * sc
-                if step < ITERS - 1:
-                    st["r"] = st["r"] - alpha * image
-                    new = dots(st["r"], st["r"])
-                    st["p"] = st["r"] + new / st["rr"] * st["p"]
-                    st["rr"] = new
-        for st in work:
-            n, h = st["n"], st["h"]
-            x_ref[st["row"], lanes(h)] = st["x"]
-            near_ref[st["row"], lanes(h)] = weighted(st["acc"], vh[0, n, h], vh[1, n, h])
+                st["r"] = st["r"] - alpha * image
+                new = dots(st["r"], st["r"])
+                st["p"] = st["r"] + new / st["rr"] * st["p"]
+                st["rr"] = new
+        for lo in range(0, len(work), 4):
+            part = work[lo : lo + 4]
+            scores, images, mixes = [], [], []
+            for st in part:
+                n, h = st["n"], st["h"]
+                p_hi, p_lo = halves(st["p"])
+                scores.append(jnp.where(causal, scores_of(p_hi, p_lo, kt[0, n, h], kt[1, n, h]), 0.0))
+                images.append(narrow(p_hi, p_lo, *st["gram"]) + st["p"])
+            for st, image, sc in zip(part, images, scores):
+                n, h = st["n"], st["h"]
+                alpha = st["rr"] / energy(st["p"] * image, sc * sc)
+                st["x"] = st["x"] + alpha * st["p"]
+                mix = st["acc"] + alpha * sc
+                mixes.append(weighted(mix, vh[0, n, h], vh[1, n, h]))
+            for st, mix in zip(part, mixes):
+                x_ref[st["row"], lanes(st["h"])] = st["x"]
+                near_ref[st["row"], lanes(st["h"])] = mix
 
     groups = blocks * BLOCK // GROUP
+    send_sums(1)
     after_z(0)
-    send_sums(1)
     after_x(0)
     after_z(1)
     after_g(0)
@@ -284,11 +296,6 @@
     pl.loop(0, groups)(solve_group)
     for d in range(1, nz):
         ecopy(1, d).wait_recv()
-    for h in range(HEADS):
-        for b in range(blocks):
-            hi, lo = halves(e[1, pl.ds(h * half, half)].reshape(HEAD, HEAD) + near_s[b, h])
-            state_ref[0, b, h] = hi
-            state_ref[1, b, h] = lo
     for c in range(2):
         for d in range(1, nz):
             zcopy(c, d).wait_send()
@@ -312,7 +319,8 @@
     outs = (
         pltpu.VMEM((tokens, width), F32),
         pltpu.VMEM((tokens, width), F32),
-        pltpu.VMEM((2, blocks, HEADS, HEAD, HEAD), BF16),
+        pltpu.VMEM((nz, rows, HEAD), F32),
+        pltpu.VMEM((blocks, HEADS, HEAD, HEAD), F32),
     )
     square = pltpu.VMEM((blocks, HEADS, HEAD, HEAD), F32)
     pieces = pltpu.VMEM((2, nz, rows, HEAD), F32)
@@ -326,25 +334,25 @@
             pltpu.VMEM((tokens, width), F32),
             pltpu.VMEM((tokens, width), F32),
             pltpu.VMEM((tokens, width), F32),
-            pltpu.VMEM((blocks, HEADS, BLOCK, BLOCK), F32),
+            pltpu.VMEM((1, blocks, HEADS, BLOCK, BLOCK), F32),
             pltpu.VMEM((2, blocks, HEADS, HEAD, BLOCK), BF16),
             pltpu.VMEM((2, blocks, HEADS, BLOCK, HEAD), BF16),
             pltpu.VMEM((2, blocks, HEADS, BLOCK, HEAD), BF16),
-            square, square, square,
+            square, square,
             pieces, pieces, pieces,
             pltpu.VMEM((2, nx, rows, HEAD), F32),
             pltpu.VMEM((2, ng, rows, HEAD), F32),
-            pieces, pieces,
+            pieces, pltpu.VMEM((nz, rows, HEAD), F32),
             dma, dma((blocks,)), dma((blocks,)),
             dma((2, nz)), dma((2, nz)), dma((2, nx)), dma((2, nx)),
             dma((2, ng)), dma((2, ng)), dma((2, nz)), dma((2, nz)),
         ],
-        compiler_params=pltpu.CompilerParams(collective_id=0, has_side_effects=True, vmem_limit_bytes=63_400_000),
+        compiler_params=pltpu.CompilerParams(collective_id=0, has_side_effects=True, vmem_limit_bytes=63_300_000),
         name="steps",
     )(queries, keys, values)
 
 
-def last_kernel(x_ref, near_ref, state_ref, out_ref):
+def last_kernel(x_ref, near_ref, state_ref, near_s, out_ref):
     first = lax.axis_index("grp") * lax.axis_size("seq") + lax.axis_index("seq")
     first = (first * pl.num_programs(0) + pl.program_id(0)) * GROUP
     for c in range(GROUP // BLOCK):
@@ -353,7 +361,9 @@
         place = (first + c * BLOCK + lax.broadcasted_iota(jnp.int32, (BLOCK, HEAD), 0)).astype(F32)
         scale = jnp.sqrt(place + 1.0)
         for h in range(HEADS):
-            out = narrow(*halves(x_ref[row, lanes(h)]), state_ref[0, n, h], state_ref[1, n, h])
+            half = state_ref.shape[0] // HEADS
+            state = halves(state_ref[pl.ds(h * half, half)].reshape(HEAD, HEAD) + near_s[n, h])
+            out = narrow(*halves(x_ref[row, lanes(h)]), *state)
             out_ref[pl.ds(c * BLOCK, BLOCK), lanes(h)] = (out + near_ref[row, lanes(h)]) * scale
 
 

time: 34.8 us -> 34.6 us (level)
  no operation moved by 1% of the time
where the time goes in v6:
time: 34.6 us; the launch traced here: 34.5 us
  Pallas kernels  34.5 us (100%)
    pallas_call x1, Pallas kernels, steps(): pl.pallas_call(functools.partial(main_kernel, nz), out_shape=outs, in_spe...  33 us
    pallas_call x1, Pallas kernels, last(): pl.pallas_call(last_kernel, grid=(tokens // GROUP,), out_shape=jax.ShapeD...  1.49 us

profile of v6, /device:TPU:24, one launch (start us, length us, event | category | flops | bytes accessed | tf_op | source)
XLA Modules:
  0.0 34.5 jit_solution(16333814645487367451)
XLA Ops:
  0.0 33.0 %steps.1 = (f32[1024,256]{1,0:T(8,128)S(1)}, f32[1024,256]{1,0:T(8,128)S(1)}, f32[8,32,128]{2,1,0:T(8,128)S(1)}, f32[4,2,128,128]{3,2,1,0:T(8,128)S(1)}) custom-call(f32[1024,256]{1,0:T(8,128)} %q_hbm.1, f32[1024,256]{1,0:T(8,128)} %k_hbm.1, f32[1024,256]{1,0:T(8,128)} %v_hbm.1), custom_call_target="tpu_custom_call" | custom-call | tf_op jit(solution)/shard_map/steps/pallas_call | solution.py:327
  33.0 1.5 %last.1 = f32[1024,256]{1,0:T(8,128)} custom-call(f32[1024,256]{1,0:T(8,128)S(1)} %get-tuple-element.9.x_ref, f32[1024,256]{1,0:T(8,128)S(1)} %get-tuple-element.10.near_ref, f32[8,32,128]{2,1,0:T(8,128)S(1)} %get-tuple-element.11.state_ref, f32[4,2,128,128]{3,2,1,0:T(8,128)S(1)} %get-tuple-element.12.near_s), custom_call_target="tpu_custom_call" | custom-call | tf_op jit(solution)/shard_map/last/pallas_call | solution.py:372

commit v7 on v6

--- a/solution.py
+++ b/solution.py
@@ -200,7 +200,7 @@
             zpre[c, j] = run
             run = run + zin[c, j]
         xin[c, x] = run
-        for d in range(1, nx):
+        for d in sorted(range(1, nx), key=lambda d: -min(d, nx - d)):
             xcopy(c, d).start()
 
     def after_x(c):
@@ -213,7 +213,7 @@
             whole = whole + piece
         held[c] = before
         gin[c, g] = whole
-        for d in range(1, ng):
+        for d in sorted(range(1, ng), key=lambda d: -min(d, ng - d)):
             @pl.when(g + d < ng)
             def _():
                 gcopy(c, d).start()
@@ -291,6 +291,15 @@
     after_x(1)
     pl.loop(AHEAD, blocks)(local_part)
     after_g(1)
+    for c in range(2):
+        for d in range(1, nz):
+            zcopy(c, d).wait_send()
+        for d in range(1, nx):
+            xcopy(c, d).wait_send()
+        for d in range(1, ng):
+            @pl.when(g + d < ng)
+            def _():
+                gcopy(c, d).wait_send()
     for d in range(1, nz):
         ecopy(0, d).wait_recv()
     pl.loop(0, groups)(solve_group)
@@ -298,14 +307,7 @@
         ecopy(1, d).wait_recv()
     for c in range(2):
         for d in range(1, nz):
-            zcopy(c, d).wait_send()
             ecopy(c, d).wait_send()
-        for d in range(1, nx):
-            xcopy(c, d).wait_send()
-        for d in range(1, ng):
-            @pl.when(g + d < ng)
-            def _():
-                gcopy(c, d).wait_send()
 
 
 def steps(queries, keys, values, nz):

time: 34.6 us -> 34.3 us (level)
  no operation moved by 1% of the time
where the time goes in v7:
time: 34.3 us; the launch traced here: 34.2 us
  Pallas kernels  34.2 us (100%)
    pallas_call x1, Pallas kernels, steps(): pl.pallas_call(functools.partial(main_kernel, nz), out_shape=outs, in_spe...  32.7 us
    pallas_call x1, Pallas kernels, last(): pl.pallas_call(last_kernel, grid=(tokens // GROUP,), out_shape=jax.ShapeD...  1.49 us

profile of v7, /device:TPU:24, one launch (start us, length us, event | category | flops | bytes accessed | tf_op | source)
XLA Modules:
  0.0 34.2 jit_solution(4145663794838556270)
XLA Ops:
  0.0 32.7 %steps.1 = (f32[1024,256]{1,0:T(8,128)S(1)}, f32[1024,256]{1,0:T(8,128)S(1)}, f32[8,32,128]{2,1,0:T(8,128)S(1)}, f32[4,2,128,128]{3,2,1,0:T(8,128)S(1)}) custom-call(f32[1024,256]{1,0:T(8,128)} %q_hbm.1, f32[1024,256]{1,0:T(8,128)} %k_hbm.1, f32[1024,256]{1,0:T(8,128)} %v_hbm.1), custom_call_target="tpu_custom_call" | custom-call | tf_op jit(solution)/shard_map/steps/pallas_call | solution.py:329
  32.8 1.5 %last.1 = f32[1024,256]{1,0:T(8,128)} custom-call(f32[1024,256]{1,0:T(8,128)S(1)} %get-tuple-element.9.x_ref, f32[1024,256]{1,0:T(8,128)S(1)} %get-tuple-element.10.near_ref, f32[8,32,128]{2,1,0:T(8,128)S(1)} %get-tuple-element.11.state_ref, f32[4,2,128,128]{3,2,1,0:T(8,128)S(1)} %get-tuple-element.12.near_s), custom_call_target="tpu_custom_call" | custom-call | tf_op jit(solution)/shard_map/last/pallas_call | solution.py:374

commit v8 on v7

--- a/solution.py
+++ b/solution.py
@@ -72,7 +72,7 @@
 
 def main_kernel(
     nz, q_hbm, k_hbm, v_hbm, x_ref, near_ref, state_ref, near_s,
-    qbuf, kbuf, vbuf, img, s_ref, kt, kh, vh, near_a, near_b,
+    qbuf, qh, kbuf, vbuf, img, s_ref, kt, kh, vh, near_a, near_b,
     sums, zin, zpre, xin, gin, eout, e,
     qsem, ksem, vsem, zs, zr, xs, xr, gs, gr, es, er,
 ):
@@ -177,6 +177,8 @@
         for h in range(HEADS):
             q = qbuf[row, lanes(h)]
             q_hi, q_lo = halves(q)
+            qh[0, row, lanes(h)] = q_hi
+            qh[1, row, lanes(h)] = q_lo
             kt_hi, kt_lo = halves(kbuf[row, lanes(h)].T)
             kt[0, b, h] = kt_hi
             kt[1, b, h] = kt_lo
@@ -235,7 +237,7 @@
         work = []
         every = pl.ds(pl.multiple_of(i * GROUP, GROUP), GROUP)
         enter = [e[pl.ds(h * half, half)].reshape(HEAD, HEAD) for h in range(HEADS)]
-        far = [narrow(*halves(qbuf[every, lanes(h)]), *halves(enter[h])) for h in range(HEADS)]
+        far = [narrow(qh[0, every, lanes(h)], qh[1, every, lanes(h)], *halves(enter[h])) for h in range(HEADS)]
         for c in range(GROUP // BLOCK):
             for h in range(HEADS):
                 n = i * (GROUP // BLOCK) + c
@@ -333,6 +335,7 @@
         out_specs=(vmem,) * len(outs),
         scratch_shapes=[
             pltpu.VMEM((tokens, width), F32),
+            pltpu.VMEM((2, tokens, width), BF16),
             pltpu.VMEM((tokens, width), F32),
             pltpu.VMEM((tokens, width), F32),
             pltpu.VMEM((tokens, width), F32),

time: 34.3 us -> 34.3 us (level)
  no operation moved by 1% of the time
where the time goes in v8:
time: 34.3 us
  Pallas kernels  34.2 us (100%)
    pallas_call x1, Pallas kernels, steps(): pl.pallas_call(functools.partial(main_kernel, nz), out_shape=outs, in_spe...  32.8 us
    pallas_call x1, Pallas kernels, last(): pl.pallas_call(last_kernel, grid=(tokens // GROUP,), out_shape=jax.ShapeD...  1.49 us

profile of v8, /device:TPU:24, one launch (start us, length us, event | category | flops | bytes accessed | tf_op | source)
XLA Modules:
  0.0 34.3 jit_solution(14363810485994402251)
XLA Ops:
  0.0 32.8 %steps.1 = (f32[1024,256]{1,0:T(8,128)S(1)}, f32[1024,256]{1,0:T(8,128)S(1)}, f32[8,32,128]{2,1,0:T(8,128)S(1)}, f32[4,2,128,128]{3,2,1,0:T(8,128)S(1)}) custom-call(f32[1024,256]{1,0:T(8,128)} %q_hbm.1, f32[1024,256]{1,0:T(8,128)} %k_hbm.1, f32[1024,256]{1,0:T(8,128)} %v_hbm.1), custom_call_target="tpu_custom_call" | custom-call | tf_op jit(solution)/shard_map/steps/pallas_call | solution.py:331
  32.8 1.5 %last.1 = f32[1024,256]{1,0:T(8,128)} custom-call(f32[1024,256]{1,0:T(8,128)S(1)} %get-tuple-element.9.x_ref, f32[1024,256]{1,0:T(8,128)S(1)} %get-tuple-element.10.near_ref, f32[8,32,128]{2,1,0:T(8,128)S(1)} %get-tuple-element.11.state_ref, f32[4,2,128,128]{3,2,1,0:T(8,128)S(1)} %get-tuple-element.12.near_s), custom_call_target="tpu_custom_call" | custom-call | tf_op jit(solution)/shard_map/last/pallas_call | solution.py:377
